TPU v7x, 32 devices: a whole 2x2x4 slice. The times are simulated.
32 devices in a mesh: group: 2 (over y), gx: 4 (over z), gy: 2 (over x), sec: 2 (over core).
Axes of the slice: x: 2, y: 2, z: 4, core: 2. Of those that a mesh axis runs over, the one named last changes fastest.
Arguments:
- pressure: float32 [2, 32, 32, 128], P('sec', ('group', 'gx'), 'gy'), parts along dimension 1, may hold values from -6 to 6
- pressure_before: float32 [2, 32, 32, 128], P('sec', ('group', 'gx'), 'gy'), parts along dimension 1, may hold values from -6 to 6
- quasi: float32 [2, 32, 32, 128], P('sec', ('group', 'gx'), 'gy'), parts along dimension 1, may hold values from -6 to 6
- quasi_before: float32 [2, 32, 32, 128], P('sec', ('group', 'gx'), 'gy'), parts along dimension 1, may hold values from -6 to 6
- courant: float32 [16, 32, 128], P('gx', 'gy'), may hold values from 0.02 to 0.08
- epsilon: float32 [16, 32, 128], P('gx', 'gy'), may hold values from 0 to 0.3
- delta: float32 [16, 32, 128], P('gx', 'gy'), may hold values from -0.1 to 0.2
- tilt: float32 [16, 32, 128], P('gx', 'gy'), may hold values from -3.140625 to 3.140625
- azimuth: float32 [16, 32, 128], P('gx', 'gy'), may hold values from -3.140625 to 3.140625
- plan: int32 [4], replicated, may hold values from 1 to 8, as said below
- lags: int32 [5], replicated, may hold values from -4 to 4, as said below
Outputs:
- pressure_final: float32 [2, 32, 32, 128], P('sec', ('group', 'gx'), 'gy'), parts along dimension 1
- quasi_final: float32 [2, 32, 32, 128], P('sec', ('group', 'gx'), 'gy'), parts along dimension 1
- image: float32 [5, 32, 32, 128], P(None, ('group', 'gx'), 'gy', 'sec'), parts along dimension 1
There are 2 independent parts, one for each index of `group`. A program takes and returns all parts, laid end to end along the dimension named above; an argument that names none is the same for every part. Nothing has to cross between parts.
Inputs may be any that keep to these rules, and one draw needn't show every extreme that they name: `plan`: distinct steps in rising order; the last entry is 8. Distinct lags; the first is -4 and the last 4.
All inputs are finite; a program needn't handle non-finite values.
Results may differ from a plain program's by a relative error of at most 0.0001.
Values sent between devices are 32-bit elements; how exact they have to be, the bound alone decides.
A program may use at most 64 MiB of HBM per device.

v0:
```python
import functools

import jax
import jax.numpy as jnp
from jax import lax
from jax.experimental import pallas as pl
from jax.experimental.pallas import tpu as pltpu
from jax.sharding import PartitionSpec as P

STEPS = 8
REACH = 4
LEAD = 8

SECOND = (-205.0 / 72.0, 8.0 / 5.0, -1.0 / 5.0, 8.0 / 315.0, -1.0 / 560.0)
FIRST = (4.0 / 5.0, -1.0 / 5.0, 4.0 / 105.0, -1.0 / 280.0)
MESH = pl.DeviceIdType.MESH
WAYS = ((0, -1), (0, 1), (-1, 0), (1, 0), (-1, -1), (-1, 1), (1, -1), (1, 1))


def first_of(at):
    result = FIRST[0] * (at(1) - at(-1))
    for m in range(2, 5):
        result = result + FIRST[m - 1] * (at(m) - at(-m))
    return result


def second_of(at):
    result = SECOND[0] * at(0)
    for m in range(1, 5):
        result = result + SECOND[m] * (at(m) + at(-m))
    return result


def kernel(
    shape, p_in, pb_in, q_in, qb_in, courant, epsilon, delta, tilt, azimuth, plan, lags,
    p_out, q_out, image,
    field, edge_out, edge_in, other, weight, partial, slope, send, recv, send_sec, recv_sec,
):
    nx, ny = shape
    ix, iy, sec = lax.axis_index("gx"), lax.axis_index("gy"), lax.axis_index("sec")
    X, Y, Z = p_in.shape[1:]
    rows = pl.ds(LEAD, Y)

    def exists(dx, dy):
        ok = (ix + dx >= 0) & (ix + dx < nx) & (iy + dy >= 0) & (iy + dy < ny)
        return ok

    def copy(slot, k):
        dx, dy = WAYS[k]
        if dy == 0:
            start, land = (X, 0) if dx > 0 else (REACH, X + REACH)
            src = field.at[slot, :, pl.ds(start, REACH), rows, :]
            dst = field.at[slot, :, pl.ds(land, REACH), rows, :]
        else:
            side = 0 if dy > 0 else 1
            start, land, many = {0: (0, REACH, X), 1: (X - REACH, 0, REACH), -1: (0, X + REACH, REACH)}[dx]
            src = edge_out.at[slot, side, pl.ds(start, many)]
            dst = edge_in.at[slot, side, pl.ds(land, many)]
        return pltpu.make_async_remote_copy(
            src_ref=src, dst_ref=dst, send_sem=send.at[slot, k], recv_sem=recv.at[slot, k],
            device_id={"gx": ix + dx, "gy": iy + dy}, device_id_type=MESH)

    def last_copy(k):
        dx, dy = WAYS[k]
        start, land = (X, 0) if dx > 0 else (REACH, X + REACH)
        last = STEPS + 1
        return pltpu.make_async_remote_copy(
            src_ref=field.at[last, 0, pl.ds(start, REACH), rows, :],
            dst_ref=field.at[last, 0, pl.ds(land, REACH), rows, :],
            send_sem=send.at[last, k], recv_sem=recv.at[last, k],
            device_id={"gx": ix + dx, "gy": iy}, device_id_type=MESH)

    def share(slot):
        return pltpu.make_async_remote_copy(
            src_ref=field.at[slot, 0, :, rows, :], dst_ref=other.at[slot],
            send_sem=send_sec.at[slot], recv_sem=recv_sec.at[slot],
            device_id={"sec": 1 - sec}, device_id_type=MESH)

    def start_all(slot):
        for k in (2, 3, 4, 5, 6, 7, 0, 1):
            @pl.when(exists(*WAYS[k]))
            def _():
                copy(slot, k).start()

    def await_from(slot, ks):
        for k in ks:
            dx, dy = WAYS[k]

            @pl.when(exists(-dx, -dy))
            def _():
                copy(slot, k).wait_recv()

    barrier = pltpu.get_barrier_semaphore()
    for dx, dy in WAYS:
        @pl.when(exists(dx, dy))
        def _():
            pl.semaphore_signal(barrier, inc=1, device_id={"gx": ix + dx, "gy": iy + dy}, device_id_type=MESH)
    pl.semaphore_signal(barrier, inc=1, device_id={"sec": 1 - sec}, device_id_type=MESH)

    def put_edges(slot, x, p, q):
        edge_out[slot, 0, x, 0:REACH] = q[Y - REACH:]
        edge_out[slot, 0, x, REACH:] = p[Y - REACH:]
        edge_out[slot, 1, x, 0:REACH] = p[:REACH]
        edge_out[slot, 1, x, REACH:] = q[:REACH]

    for x in range(X):
        p, q = p_in[0, x], q_in[0, x]
        field[1, 0, REACH + x, LEAD:LEAD + Y] = p
        field[1, 1, REACH + x, LEAD:LEAD + Y] = q
        put_edges(1, x, p, q)
        field[0, 0, REACH + x, LEAD:LEAD + Y] = pb_in[0, x]
        field[0, 1, REACH + x, LEAD:LEAD + Y] = qb_in[0, x]

    pl.semaphore_wait(barrier, 1 + sum(exists(*way).astype(jnp.int32) for way in WAYS))
    start_all(1)

    for beyond, at in ((ix == 0, 0), (ix == nx - 1, X + REACH)):
        @pl.when(beyond)
        def _():
            @pl.loop(1, STEPS + 2)
            def _(slot):
                field[slot, :, at:at + REACH, LEAD:LEAD + Y] = jnp.zeros((2, REACH, Y, Z), jnp.float32)
                edge_in[slot, :, at:at + REACH] = jnp.zeros((2, REACH, 8, Z), jnp.float32)
    for beyond, side in ((iy == 0, 0), (iy == ny - 1, 1)):
        @pl.when(beyond)
        def _():
            @pl.loop(1, STEPS + 2)
            def _(slot):
                edge_in[slot, side] = jnp.zeros((X + 2 * REACH, 8, Z), jnp.float32)

    for x in range(X):
        t, a, c = tilt[x], azimuth[x], courant[x]
        st, ct, sa, ca = jnp.sin(t), jnp.cos(t), jnp.sin(a), jnp.cos(a)
        square, double = st * st, 2.0 * st * ct
        weight[0, x] = square * ca * ca
        weight[1, x] = square * sa * sa
        weight[2, x] = ct * ct
        weight[3, x] = square * (2.0 * sa * ca)
        weight[4, x] = double * sa
        weight[5, x] = double * ca
        weight[6, x] = c * (1.0 + 2.0 * epsilon[x])
        weight[7, x] = c * (1.0 + 2.0 * delta[x])

    lane = lax.broadcasted_iota(jnp.int32, (Y, Z), 1)
    inside = {m: (lane + m >= 0) & (lane + m < Z) for m in range(-4, 5) if m}

    def along_z(value):
        def at(m):
            if m == 0:
                return value
            return jnp.where(inside[m], pltpu.roll(value, (-m) % Z, 1), 0.0)
        return at

    @pl.loop(1, STEPS + 1)
    def _(cur):
        def blend(f, i, x):
            w = weight[i, x]
            if f == 1:
                return w
            return 1.0 - w if i < 3 else -w

        for f in range(2):
            for x in range(X):
                value = field[cur, f, REACH + x, LEAD:LEAD + Y]
                partial[f, x] = blend(f, 2, x) * second_of(along_z(value))

        def open_edges(x):
            low, high = edge_in[cur, 0, x], edge_in[cur, 1, x]
            field[cur, 0, x, LEAD - REACH:LEAD] = low[REACH:]
            field[cur, 1, x, LEAD - REACH:LEAD] = low[:REACH]
            field[cur, 0, x, LEAD + Y:LEAD + Y + REACH] = high[:REACH]
            field[cur, 1, x, LEAD + Y:LEAD + Y + REACH] = high[REACH:]

        await_from(cur, (0, 1))
        for x in range(X):
            open_edges(REACH + x)
        for f in range(2):
            for x in range(X):
                def at_y(m):
                    return field[cur, f, REACH + x, LEAD + m:LEAD + m + Y]
                total = partial[f, x] + blend(f, 1, x) * second_of(at_y)
                partial[f, x] = total + blend(f, 4, x) * first_of(along_z(first_of(at_y)))

        await_from(cur, (2, 3, 4, 5, 6, 7))

        @pl.when(cur > 1)
        def _():
            share(cur).start()

        for x in range(REACH):
            open_edges(x)
            open_edges(X + REACH + x)
        for x in range(X):
            both = []
            for f in range(2):
                def at_x(m):
                    return field[cur, f, REACH + x + m, LEAD:LEAD + Y]

                def at_x_wide(m):
                    return field[cur, f, REACH + x + m, LEAD - REACH:LEAD + Y + REACH]
                total = partial[f, x] + blend(f, 0, x) * second_of(at_x)
                slope[f, x] = first_of(at_x_wide)
                total = total + blend(f, 5, x) * first_of(along_z(slope[f, x, REACH:REACH + Y]))
                both.append(total + blend(f, 3, x) * first_of(
                    lambda m: slope[f, x, REACH + m:REACH + m + Y]))
            h2p, h1q = both
            push = courant[x] * h1q
            p = 2.0 * field[cur, 0, REACH + x, LEAD:LEAD + Y] - field[cur - 1, 0, REACH + x, LEAD:LEAD + Y]
            q = 2.0 * field[cur, 1, REACH + x, LEAD:LEAD + Y] - field[cur - 1, 1, REACH + x, LEAD:LEAD + Y]
            p = p + (weight[6, x] * h2p + push)
            q = q + (weight[7, x] * h2p + push)
            field[cur + 1, 0, REACH + x, LEAD:LEAD + Y] = p
            field[cur + 1, 1, REACH + x, LEAD:LEAD + Y] = q
            put_edges(cur + 1, x, p, q)

        @pl.when(cur < STEPS)
        def _():
            start_all(cur + 1)

    last = STEPS + 1
    for k in (2, 3):
        @pl.when(exists(*WAYS[k]))
        def _():
            last_copy(k).start()
    for x in range(X):
        p_out[0, x] = field[last, 0, REACH + x, LEAD:LEAD + Y]
        q_out[0, x] = field[last, 1, REACH + x, LEAD:LEAD + Y]
    for k in (2, 3):
        @pl.when(exists(-WAYS[k][0], 0))
        def _():
            last_copy(k).wait_recv()
    share(last).start()

    @pl.loop(2, STEPS + 2)
    def _(slot):
        share(slot).wait_recv()

    turn = 1 - 2 * sec
    half = Z // 2
    for i in range(lags.shape[0]):
        shift = lags[i] * turn
        for x in range(X):
            total = None
            for j in range(plan.shape[0]):
                slot = plan[j] + 1
                term = field[slot, 0, REACH + x - shift, LEAD:LEAD + Y] * other[slot, REACH + x + shift]
                total = term if total is None else total + term
            image[i, x] = jnp.where(sec == 0, total, pltpu.roll(total, half, 1))[:, :half]

    @pl.loop(1, STEPS + 1)
    def _(slot):
        for k in range(len(WAYS)):
            @pl.when(exists(*WAYS[k]))
            def _():
                copy(slot, k).wait_send()
    for k in (2, 3):
        @pl.when(exists(*WAYS[k]))
        def _():
            last_copy(k).wait_send()

    @pl.loop(2, STEPS + 2)
    def _(slot):
        share(slot).wait_send()


def on_device(mesh_shape, *args):
    p, plan, lags = args[0], args[9], args[10]
    X, Y, Z = p.shape[1:]
    slots, wide = STEPS + 2, X + 2 * REACH
    dma = pltpu.SemaphoreType.DMA
    vmem, smem = pl.BlockSpec(memory_space=pltpu.VMEM), pl.BlockSpec(memory_space=pltpu.SMEM)
    return pl.pallas_call(
        functools.partial(kernel, mesh_shape),
        out_shape=(
            jax.ShapeDtypeStruct(p.shape, jnp.float32),
            jax.ShapeDtypeStruct(p.shape, jnp.float32),
            jax.ShapeDtypeStruct((lags.shape[0], X, Y, Z // 2), jnp.float32),
        ),
        in_specs=[vmem] * 9 + [smem] * 2,
        out_specs=(vmem, vmem, vmem),
        scratch_shapes=[
            pltpu.VMEM((slots, 2, wide, Y + 2 * LEAD, Z), jnp.float32),
            pltpu.VMEM((slots, 2, X, 8, Z), jnp.float32),
            pltpu.VMEM((slots, 2, wide, 8, Z), jnp.float32),
            pltpu.VMEM((slots, wide, Y, Z), jnp.float32),
            pltpu.VMEM((8, X, Y, Z), jnp.float32),
            pltpu.VMEM((2, X, Y, Z), jnp.float32),
            pltpu.VMEM((2, X, Y + 2 * REACH, Z), jnp.float32),
            dma((slots, len(WAYS))),
            dma((slots, len(WAYS))),
            dma((slots,)),
            dma((slots,)),
        ],
        compiler_params=pltpu.CompilerParams(collective_id=0, has_side_effects=True),
        name="steps",
    )(*args)


def solution(mesh):
    field, medium = P("sec", ("group", "gx"), "gy", None), P("gx", "gy", None)
    return jax.shard_map(
        functools.partial(on_device, (mesh.shape["gx"], mesh.shape["gy"])),
        mesh=mesh,
        in_specs=(field,) * 4 + (medium,) * 5 + (P(), P()),
        out_specs=(field, field, P(None, ("group", "gx"), "gy", "sec")),
        check_vma=False,
    )
```

profile of v0, /device:TPU:0, one launch (start us, length us, event | category | flops | bytes accessed | tf_op | source)
XLA Modules:
  0.0 51.1 jit_solution(541017618437301207)
XLA Ops:
  0.6 46.8 %steps.1 = (f32[1,4,16,128]{3,2,1,0:T(8,128)}, f32[1,4,16,128]{3,2,1,0:T(8,128)}, f32[5,4,16,64]{3,2,1,0:T(8,128)}) custom-call(f32[1,4,16,128]{3,2,1,0:T(8,128)} %p_in.1, f32[1,4,16,128]{3,2,1,0:T(8,128)} %pb_in.1, f32[1,4,16,128]{3,2,1,0:T(8,128)} %q_in.1, f32[1,4,16,128]{3,2,1,0:T(8,128)} %qb_in.1, f32[4,16,128]{2,1,0:T(8,128)} %courant.1, ...), custom_call_target="tpu_custom_call" | custom-call | tf_op jit(solution)/shard_map/steps/pallas_call | solution.py:272
  47.5 0.0 copy-start
  47.5 1.4 %copy.17 = f32[1,4,16,128]{3,2,1,0:T(8,128)} copy(f32[1,4,16,128]{3,2,1,0:T(8,128)} %get-tuple-element.6) | data formatting | bytes 65536
  48.9 0.0 copy-done
  48.9 0.6 %copy.18 = f32[1,4,16,128]{3,2,1,0:T(8,128)} copy(f32[1,4,16,128]{3,2,1,0:T(8,128)S(1)} %copy-done) | data formatting | bytes 65536
  49.5 1.6 %copy.19 = f32[5,4,16,64]{3,2,1,0:T(8,128)} copy(f32[5,4,16,64]{3,2,1,0:T(8,128)} %get-tuple-element.8) | data formatting | bytes 163840
Async XLA Ops:
  47.5 1.4 %copy-start = (f32[1,4,16,128]{3,2,1,0:T(8,128)S(1)}, f32[1,4,16,128]{3,2,1,0:T(8,128)}, u32[]{:S(2)}) copy-start(f32[1,4,16,128]{3,2,1,0:T(8,128)} %get-tuple-element.7) | copy-start | bytes 98308
where the time goes:
time: 51.6 us; the launch traced here: 51.1 us
  Pallas kernels  46.8 us (91%)
  local copies, waits for them, and re-layouts  3.59 us (7%)
  between operations  0.65 us (1%)
    pallas_call x1, Pallas kernels, on_device(): pl.pallas_call(functools.partial(kernel, mesh_shape), out_shape=(jax.Shap...  46.8 us
    unnamed x5, local copies, waits for them, and re-layouts  3.59 us

commit v1 on v0

--- a/solution.py
+++ b/solution.py
@@ -10,6 +10,7 @@
 STEPS = 8
 REACH = 4
 LEAD = 8
+PIECE = 4
 
 SECOND = (-205.0 / 72.0, 8.0 / 5.0, -1.0 / 5.0, 8.0 / 315.0, -1.0 / 560.0)
 FIRST = (4.0 / 5.0, -1.0 / 5.0, 4.0 / 105.0, -1.0 / 280.0)
@@ -34,7 +35,7 @@
 def kernel(
     shape, p_in, pb_in, q_in, qb_in, courant, epsilon, delta, tilt, azimuth, plan, lags,
     p_out, q_out, image,
-    field, edge_out, edge_in, other, weight, partial, slope, send, recv, send_sec, recv_sec,
+    field, edge_out, edge_in, other, weight, partial, slope, stacked, tail, send, recv, send_sec, recv_sec,
 ):
     nx, ny = shape
     ix, iy, sec = lax.axis_index("gx"), lax.axis_index("gy"), lax.axis_index("sec")
@@ -45,30 +46,38 @@
         ok = (ix + dx >= 0) & (ix + dx < nx) & (iy + dy >= 0) & (iy + dy < ny)
         return ok
 
-    def copy(slot, k):
+    def copy(slot, k, c):
         dx, dy = WAYS[k]
+        begin, many = c * PIECE, PIECE
+        if dx == 0:
+            start, land, begin, many = 0, REACH, 0, X
+        elif dx > 0:
+            start, land = X - REACH, 0
+        else:
+            start, land = 0, X + REACH
         if dy == 0:
-            start, land = (X, 0) if dx > 0 else (REACH, X + REACH)
-            src = field.at[slot, :, pl.ds(start, REACH), rows, :]
-            dst = field.at[slot, :, pl.ds(land, REACH), rows, :]
+            src = field.at[slot, :, pl.ds(REACH + start + begin, many), rows, :]
+            dst = field.at[slot, :, pl.ds(land + begin, many), rows, :]
         else:
             side = 0 if dy > 0 else 1
-            start, land, many = {0: (0, REACH, X), 1: (X - REACH, 0, REACH), -1: (0, X + REACH, REACH)}[dx]
-            src = edge_out.at[slot, side, pl.ds(start, many)]
-            dst = edge_in.at[slot, side, pl.ds(land, many)]
+            src = edge_out.at[slot, side, pl.ds(start + begin, many)]
+            dst = edge_in.at[slot, side, pl.ds(land + begin, many)]
         return pltpu.make_async_remote_copy(
-            src_ref=src, dst_ref=dst, send_sem=send.at[slot, k], recv_sem=recv.at[slot, k],
+            src_ref=src, dst_ref=dst, send_sem=send.at[slot, k, c], recv_sem=recv.at[slot, k, c],
             device_id={"gx": ix + dx, "gy": iy + dy}, device_id_type=MESH)
 
-    def last_copy(k):
-        dx, dy = WAYS[k]
+    def pieces(k):
+        return range(REACH // PIECE if WAYS[k][0] else 1)
+
+    last = STEPS + 1
+
+    def last_copy(k, cross):
+        dx = WAYS[k][0]
         start, land = (X, 0) if dx > 0 else (REACH, X + REACH)
-        last = STEPS + 1
         return pltpu.make_async_remote_copy(
-            src_ref=field.at[last, 0, pl.ds(start, REACH), rows, :],
-            dst_ref=field.at[last, 0, pl.ds(land, REACH), rows, :],
-            send_sem=send.at[last, k], recv_sem=recv.at[last, k],
-            device_id={"gx": ix + dx, "gy": iy}, device_id_type=MESH)
+            src_ref=tail.at[0, pl.ds(start, REACH)], dst_ref=tail.at[int(cross), pl.ds(land, REACH)],
+            send_sem=send.at[last, k + 2 * cross, 0], recv_sem=recv.at[last, k + 2 * cross, 0],
+            device_id={"gx": ix + dx, "sec": 1 - sec if cross else sec}, device_id_type=MESH)
 
     def share(slot):
         return pltpu.make_async_remote_copy(
@@ -76,11 +85,21 @@
             send_sem=send_sec.at[slot], recv_sem=recv_sec.at[slot],
             device_id={"sec": 1 - sec}, device_id_type=MESH)
 
-    def start_all(slot):
-        for k in (2, 3, 4, 5, 6, 7, 0, 1):
-            @pl.when(exists(*WAYS[k]))
-            def _():
-                copy(slot, k).start()
+    def last_share():
+        return pltpu.make_async_remote_copy(
+            src_ref=tail.at[0, pl.ds(REACH, X)], dst_ref=tail.at[1, pl.ds(REACH, X)],
+            send_sem=send_sec.at[last], recv_sem=recv_sec.at[last],
+            device_id={"sec": 1 - sec}, device_id_type=MESH)
+
+    def start_ready(slot, x):
+        for k in (4, 5, 6, 7, 0, 1, 2, 3):
+            dx = WAYS[k][0]
+            for c in pieces(k):
+                end = X - 1 if dx == 0 else (c + 1) * PIECE - 1 + (X - REACH if dx > 0 else 0)
+                if end == x:
+                    @pl.when(exists(*WAYS[k]))
+                    def _():
+                        copy(slot, k, c).start()
 
     def await_from(slot, ks):
         for k in ks:
@@ -88,13 +107,18 @@
 
             @pl.when(exists(-dx, -dy))
             def _():
-                copy(slot, k).wait_recv()
+                for c in pieces(k):
+                    copy(slot, k, c).wait_recv()
 
     barrier = pltpu.get_barrier_semaphore()
     for dx, dy in WAYS:
         @pl.when(exists(dx, dy))
         def _():
             pl.semaphore_signal(barrier, inc=1, device_id={"gx": ix + dx, "gy": iy + dy}, device_id_type=MESH)
+    for dx in (-1, 1):
+        @pl.when(exists(dx, 0))
+        def _():
+            pl.semaphore_signal(barrier, inc=1, device_id={"gx": ix + dx, "sec": 1 - sec}, device_id_type=MESH)
     pl.semaphore_signal(barrier, inc=1, device_id={"sec": 1 - sec}, device_id_type=MESH)
 
     def put_edges(slot, x, p, q):
@@ -111,12 +135,15 @@
         field[0, 0, REACH + x, LEAD:LEAD + Y] = pb_in[0, x]
         field[0, 1, REACH + x, LEAD:LEAD + Y] = qb_in[0, x]
 
-    pl.semaphore_wait(barrier, 1 + sum(exists(*way).astype(jnp.int32) for way in WAYS))
-    start_all(1)
+    pl.semaphore_wait(barrier, 1 + sum(exists(*way).astype(jnp.int32) for way in WAYS + ((-1, 0), (1, 0))))
+    for x in range(X):
+        start_ready(1, x)
 
     for beyond, at in ((ix == 0, 0), (ix == nx - 1, X + REACH)):
         @pl.when(beyond)
         def _():
+            tail[:, at:at + REACH] = jnp.zeros((2, REACH, Y, Z), jnp.float32)
+
             @pl.loop(1, STEPS + 2)
             def _(slot):
                 field[slot, :, at:at + REACH, LEAD:LEAD + Y] = jnp.zeros((2, REACH, Y, Z), jnp.float32)
@@ -213,54 +240,72 @@
             field[cur + 1, 1, REACH + x, LEAD:LEAD + Y] = q
             put_edges(cur + 1, x, p, q)
 
-        @pl.when(cur < STEPS)
-        def _():
-            start_all(cur + 1)
-
-    last = STEPS + 1
-    for k in (2, 3):
-        @pl.when(exists(*WAYS[k]))
-        def _():
-            last_copy(k).start()
+            if (x + 1) % PIECE == 0 or x == X - 1 or (X - x - 1) % PIECE == 0:
+                @pl.when(cur < STEPS)
+                def _():
+                    start_ready(cur + 1, x)
+
+    for x in range(X):
+        tail[0, REACH + x] = field[last, 0, REACH + x, LEAD:LEAD + Y]
+    last_share().start()
+    for cross in (True, False):
+        for k in (2, 3):
+            @pl.when(exists(*WAYS[k]))
+            def _():
+                last_copy(k, cross).start()
     for x in range(X):
         p_out[0, x] = field[last, 0, REACH + x, LEAD:LEAD + Y]
         q_out[0, x] = field[last, 1, REACH + x, LEAD:LEAD + Y]
-    for k in (2, 3):
-        @pl.when(exists(-WAYS[k][0], 0))
-        def _():
-            last_copy(k).wait_recv()
-    share(last).start()
-
-    @pl.loop(2, STEPS + 2)
+
+    @pl.loop(2, STEPS + 1)
     def _(slot):
         share(slot).wait_recv()
 
     turn = 1 - 2 * sec
     half = Z // 2
+
+    def term(i, x, j):
+        shift = lags[i] * turn
+        if j == plan.shape[0] - 1:
+            return tail[0, REACH + x - shift] * tail[1, REACH + x + shift]
+        slot = plan[j] + 1
+        return field[slot, 0, REACH + x - shift, LEAD:LEAD + Y] * other[slot, REACH + x + shift]
+
     for i in range(lags.shape[0]):
-        shift = lags[i] * turn
         for x in range(X):
-            total = None
-            for j in range(plan.shape[0]):
-                slot = plan[j] + 1
-                term = field[slot, 0, REACH + x - shift, LEAD:LEAD + Y] * other[slot, REACH + x + shift]
-                total = term if total is None else total + term
-            image[i, x] = jnp.where(sec == 0, total, pltpu.roll(total, half, 1))[:, :half]
+            total = term(i, x, 0)
+            for j in range(1, plan.shape[0] - 1):
+                total = total + term(i, x, j)
+            stacked[i, x] = total
 
     @pl.loop(1, STEPS + 1)
     def _(slot):
         for k in range(len(WAYS)):
             @pl.when(exists(*WAYS[k]))
             def _():
-                copy(slot, k).wait_send()
-    for k in (2, 3):
-        @pl.when(exists(*WAYS[k]))
-        def _():
-            last_copy(k).wait_send()
-
-    @pl.loop(2, STEPS + 2)
+                for c in pieces(k):
+                    copy(slot, k, c).wait_send()
+
+    @pl.loop(2, STEPS + 1)
     def _(slot):
         share(slot).wait_send()
+
+    last_share().wait_recv()
+    for cross in (True, False):
+        for k in (2, 3):
+            @pl.when(exists(-WAYS[k][0], 0))
+            def _():
+                last_copy(k, cross).wait_recv()
+    for i in range(lags.shape[0]):
+        for x in range(X):
+            total = stacked[i, x] + term(i, x, plan.shape[0] - 1)
+            image[i, x] = jnp.where(sec == 0, total, pltpu.roll(total, half, 1))[:, :half]
+    for cross in (True, False):
+        for k in (2, 3):
+            @pl.when(exists(*WAYS[k]))
+            def _():
+                last_copy(k, cross).wait_send()
+    last_share().wait_send()
 
 
 def on_device(mesh_shape, *args):
@@ -272,9 +317,9 @@
     return pl.pallas_call(
         functools.partial(kernel, mesh_shape),
         out_shape=(
-            jax.ShapeDtypeStruct(p.shape, jnp.float32),
-            jax.ShapeDtypeStruct(p.shape, jnp.float32),
-            jax.ShapeDtypeStruct((lags.shape[0], X, Y, Z // 2), jnp.float32),
+            pltpu.VMEM(p.shape, jnp.float32),
+            pltpu.VMEM(p.shape, jnp.float32),
+            pltpu.VMEM((lags.shape[0], X, Y, Z // 2), jnp.float32),
         ),
         in_specs=[vmem] * 9 + [smem] * 2,
         out_specs=(vmem, vmem, vmem),
@@ -286,8 +331,10 @@
             pltpu.VMEM((8, X, Y, Z), jnp.float32),
             pltpu.VMEM((2, X, Y, Z), jnp.float32),
             pltpu.VMEM((2, X, Y + 2 * REACH, Z), jnp.float32),
-            dma((slots, len(WAYS))),
-            dma((slots, len(WAYS))),
+            pltpu.VMEM((lags.shape[0], X, Y, Z), jnp.float32),
+            pltpu.VMEM((2, wide, Y, Z), jnp.float32),
+            dma((slots, len(WAYS), REACH // PIECE)),
+            dma((slots, len(WAYS), REACH // PIECE)),
             dma((slots,)),
             dma((slots,)),
         ],

time: 51.6 us -> 44.2 us (0.86)
  Pallas kernels: 46.8 us -> 41.5 us
  local copies, waits for them, and re-layouts: 3.59 us -> 1.9 us
    pallas_call x1, Pallas kernels: 46.8 us -> 41.5 us  [on_device(): pl.pallas_call(functools.partial(kernel, mesh_shape), out_shape=(pltpu.VM...]
    unnamed x5 -> x3, local copies, waits for them, and re-layouts: 3.59 us -> 1.9 us
where the time goes in v1:
time: 44.2 us; the launch traced here: 44 us
  Pallas kernels  41.5 us (94%)
  local copies, waits for them, and re-layouts  1.9 us (4%)
  between operations  0.64 us (1%)
    pallas_call x1, Pallas kernels, on_device(): pl.pallas_call(functools.partial(kernel, mesh_shape), out_shape=(pltpu.VM...  41.5 us
    unnamed x3, local copies, waits for them, and re-layouts  1.9 us

profile of v1, /device:TPU:0, one launch (start us, length us, event | category | flops | bytes accessed | tf_op | source)
XLA Modules:
  0.0 44.0 jit_solution(718551998926433052)
XLA Ops:
  0.6 41.5 %steps.1 = (f32[1,4,16,128]{3,2,1,0:T(8,128)S(1)}, f32[1,4,16,128]{3,2,1,0:T(8,128)S(1)}, f32[5,4,16,64]{3,2,1,0:T(8,128)S(1)}) custom-call(f32[1,4,16,128]{3,2,1,0:T(8,128)} %p_in.1, f32[1,4,16,128]{3,2,1,0:T(8,128)} %pb_in.1, f32[1,4,16,128]{3,2,1,0:T(8,128)} %q_in.1, f32[1,4,16,128]{3,2,1,0:T(8,128)} %qb_in.1, f32[4,16,128]{2,1,0:T(8,128)} %courant.1, ...), custom_call_target="tpu_custom_call" | custom-call | tf_op jit(solution)/shard_map/steps/pallas_call | solution.py:317
  42.1 0.6 %copy.17 = f32[1,4,16,128]{3,2,1,0:T(8,128)} copy(f32[1,4,16,128]{3,2,1,0:T(8,128)S(1)} %get-tuple-element.3) | data formatting | bytes 65536
  42.8 0.6 %copy.18 = f32[1,4,16,128]{3,2,1,0:T(8,128)} copy(f32[1,4,16,128]{3,2,1,0:T(8,128)S(1)} %get-tuple-element.4) | data formatting | bytes 65536
  43.4 0.7 %copy.19 = f32[5,4,16,64]{3,2,1,0:T(8,128)} copy(f32[5,4,16,64]{3,2,1,0:T(8,128)S(1)} %get-tuple-element.5) | data formatting | bytes 163840

commit v2 on v1

--- a/solution.py
+++ b/solution.py
@@ -208,15 +208,16 @@
                 total = partial[f, x] + blend(f, 1, x) * second_of(at_y)
                 partial[f, x] = total + blend(f, 4, x) * first_of(along_z(first_of(at_y)))
 
-        await_from(cur, (2, 3, 4, 5, 6, 7))
-
-        @pl.when(cur > 1)
-        def _():
-            share(cur).start()
-
+        await_from(cur, (4, 5, 6, 7))
         for x in range(REACH):
             open_edges(x)
             open_edges(X + REACH + x)
+        await_from(cur, (2, 3))
+
+        @pl.when(cur > 1)
+        def _():
+            share(cur).start()
+
         for x in range(X):
             both = []
             for f in range(2):

time: 44.2 us -> 44.3 us (level)
  no operation moved by 1% of the time
where the time goes in v2:
time: 44.3 us; the launch traced here: 44.1 us
  Pallas kernels  41.6 us (94%)
  local copies, waits for them, and re-layouts  1.9 us (4%)
  between operations  0.64 us (1%)
    pallas_call x1, Pallas kernels, on_device(): pl.pallas_call(functools.partial(kernel, mesh_shape), out_shape=(pltpu.VM...  41.6 us
    unnamed x3, local copies, waits for them, and re-layouts  1.9 us

profile of v2, /device:TPU:0, one launch (start us, length us, event | category | flops | bytes accessed | tf_op | source)
XLA Modules:
  0.0 44.1 jit_solution(15636931792258568008)
XLA Ops:
  0.6 41.6 %steps.1 = (f32[1,4,16,128]{3,2,1,0:T(8,128)S(1)}, f32[1,4,16,128]{3,2,1,0:T(8,128)S(1)}, f32[5,4,16,64]{3,2,1,0:T(8,128)S(1)}) custom-call(f32[1,4,16,128]{3,2,1,0:T(8,128)} %p_in.1, f32[1,4,16,128]{3,2,1,0:T(8,128)} %pb_in.1, f32[1,4,16,128]{3,2,1,0:T(8,128)} %q_in.1, f32[1,4,16,128]{3,2,1,0:T(8,128)} %qb_in.1, f32[4,16,128]{2,1,0:T(8,128)} %courant.1, ...), custom_call_target="tpu_custom_call" | custom-call | tf_op jit(solution)/shard_map/steps/pallas_call | solution.py:318
  42.2 0.6 %copy.17 = f32[1,4,16,128]{3,2,1,0:T(8,128)} copy(f32[1,4,16,128]{3,2,1,0:T(8,128)S(1)} %get-tuple-element.3) | data formatting | bytes 65536
  42.8 0.6 %copy.18 = f32[1,4,16,128]{3,2,1,0:T(8,128)} copy(f32[1,4,16,128]{3,2,1,0:T(8,128)S(1)} %get-tuple-element.4) | data formatting | bytes 65536
  43.4 0.7 %copy.19 = f32[5,4,16,64]{3,2,1,0:T(8,128)} copy(f32[5,4,16,64]{3,2,1,0:T(8,128)S(1)} %get-tuple-element.5) | data formatting | bytes 163840
